TPU v7x, 512 devices: a whole 4x4x16 slice. The times are simulated.
512 devices in a mesh: seq: 64 (over x, z_lo, core), tp: 8 (over z_hi, y).
Axes of the slice: x: 4, y: 4, z: 16 (z_hi: 2, z_lo: 8; z = z_hi * 8 + z_lo), core: 2. Of those that a mesh axis runs over, the one named last changes fastest.
Arguments:
- stream_x: bfloat16 [8192, 4096], P('seq', 'tp'), may hold values from -6 to 6
- norm_gain: float32 [4096], replicated, may hold values from 0.1 to 1.9
- w_qkv: bfloat16 [4096, 6144], P('seq', 'tp'), may hold values from -0.09375 to 0.09375
- cache_kv: bfloat16 [2, 4096, 1024], P(None, 'seq', 'tp'), may hold values from -400 to 400
- recomp_hidden: bfloat16 [512, 4096], P('seq', 'tp'), may hold values from -6 to 6
- recomp_index: int32 [512], P('seq'), may hold values from 0 to 4095, as said below
- prefix_len: int32 [1], replicated, may hold values from 2048 to 4096
Outputs:
- attended: bfloat16 [8192, 4096], P('seq', 'tp')
Inputs may be any that keep to these rules, and one draw needn't show every extreme that they name: `recomp_index`: the entries held by index s of seq name distinct cache rows of s * 64 to s * 64 + 63.
All inputs are finite; a program needn't handle non-finite values.
Results may differ from a plain program's by a relative error of at most 0.015.
The roundings to bfloat16 on the way count: a program that leaves them out, or rounds other values in their place, can miss the bound.
Values may be sent and summed in bfloat16 or wider, within the bound.
A program may use at most 64 MiB of HBM per device.

v0:
```python
import math

import jax
import jax.numpy as jnp
from jax import lax
from jax.sharding import PartitionSpec as P

HEADS = 32
KVH = 8
HD = 128


def normed(rows, gain):
    values = rows.astype(jnp.float32)
    spread = jnp.mean(values * values, axis=-1, keepdims=True)
    return (values * lax.rsqrt(spread + 1e-05) * gain).astype(jnp.bfloat16)


def rotate(values, places):
    half = values.shape[-1] // 2
    freq = jnp.exp(-math.log(1000000.0) * jnp.arange(half, dtype=jnp.float32) * 2.0 / (2 * half))
    angle = places[:, None] * freq[None, :]
    shape = (angle.shape[0],) + (1,) * (values.ndim - 2) + (half,)
    cosine = jnp.cos(angle).reshape(shape)
    sine = jnp.sin(angle).reshape(shape)
    first = values[..., :half]
    second = values[..., half:]
    return jnp.concatenate([first * cosine - second * sine, first * sine + second * cosine], -1)


def add_rows(left, piece):
    return jnp.dot(left, piece, preferred_element_type=jnp.float32)


def per_device(stream_x, norm_gain, w_qkv, cache_kv, recomp_hidden, recomp_index, prefix_len):
    whole_x, whole_h = (
        lax.all_gather(stream_x, "tp", axis=1, tiled=True),
        lax.all_gather(recomp_hidden, "tp", axis=1, tiled=True),
    )
    normed_x = normed(whole_x, norm_gain)
    normed_h = normed(whole_h, norm_gain)
    tok_rows = normed_x.shape[0]
    redo_rows = normed_h.shape[0]
    group = HEADS // KVH
    local = w_qkv.shape[1] // ((group + 2) * HD)
    cache_rows = cache_kv.shape[1]
    seq_at = lax.axis_index("seq")
    stacked = jnp.concatenate([normed_x, normed_h], 0)
    full = add_rows(stacked, lax.all_gather(w_qkv, "seq", axis=0, tiled=True))
    full = full.reshape(tok_rows + redo_rows, local, group + 2, HD)
    query_raw = full[:tok_rows, :, :group]
    kv_part = full[:, :, group:]
    begin = prefix_len[0]
    token_ids = seq_at * tok_rows + jnp.arange(tok_rows, dtype=jnp.int32)
    places = (token_ids + begin).astype(jnp.float32)
    query = rotate(query_raw, places).astype(jnp.bfloat16)
    new_keys = rotate(kv_part[:tok_rows, :, 0], places).astype(jnp.bfloat16)
    new_values = kv_part[:tok_rows, :, 1].astype(jnp.bfloat16)
    redo_keys = rotate(kv_part[tok_rows:, :, 0], recomp_index.astype(jnp.float32)).astype(
        jnp.bfloat16
    )
    redo_values = kv_part[tok_rows:, :, 1].astype(jnp.bfloat16)
    rows_here = recomp_index - seq_at * cache_rows
    keys_c = cache_kv[0].at[rows_here].set(redo_keys.reshape(redo_rows, local * HD))
    values_c = cache_kv[1].at[rows_here].set(redo_values.reshape(redo_rows, local * HD))
    held = jnp.stack(
        [
            jnp.concatenate([new_keys.reshape(tok_rows, local * HD), keys_c], 0),
            jnp.concatenate([new_values.reshape(tok_rows, local * HD), values_c], 0),
        ]
    )
    span = tok_rows + cache_rows
    scale = 1.0 / math.sqrt(HD)

    def attend_one(carry, piece, start):
        top_old, total, accum = carry
        count = piece.shape[1]
        rows = start + jnp.arange(count, dtype=jnp.int32)
        owner = rows // span
        within = rows % span
        is_stream = within < tok_rows
        stream_pos = owner * tok_rows + within
        cache_pos = owner * cache_rows + within - tok_rows
        allowed = jnp.where(
            is_stream[None, :],
            stream_pos[None, :] <= token_ids[:, None],
            (cache_pos < begin)[None, :],
        )
        key_rows = piece[0].reshape(count, local, HD)
        value_rows = piece[1].reshape(count, local, HD)
        score = (
            jnp.einsum("tkgd,nkd->kgtn", query, key_rows, preferred_element_type=jnp.float32)
            * scale
        )
        score = jnp.where(allowed[None, None], score, -1e30)
        top_new = jnp.maximum(top_old, jnp.max(score, -1))
        weights = jnp.where(allowed[None, None], jnp.exp(score - top_new[..., None]), 0.0)
        keep = jnp.exp(top_old - top_new)
        total = total * keep + jnp.sum(weights, -1)
        accum = accum * keep[..., None] + jnp.einsum(
            "kgtn,nkd->kgtd",
            weights.astype(jnp.bfloat16),
            value_rows,
            preferred_element_type=jnp.float32,
        )
        return (top_new, total, accum)

    init = (
        jnp.full((local, group, tok_rows), -1e30, jnp.float32),
        jnp.zeros((local, group, tok_rows), jnp.float32),
        jnp.zeros((local, group, tok_rows, HD), jnp.float32),
    )
    carry = init
    piece = lax.all_gather(held, "seq", axis=1, tiled=True)
    count = piece.shape[1]
    shards = count // span
    pieces = jnp.transpose(piece.reshape(2, shards, span, piece.shape[2]), (1, 0, 2, 3))

    def step(state, item):
        index, single = item
        return (attend_one(state, single, index * span), None)

    carry, unused = lax.scan(step, carry, (jnp.arange(shards, dtype=jnp.int32), pieces))
    top_all, total, accum = carry
    mixed = accum / total[..., None]
    return (
        jnp.transpose(mixed, (2, 0, 1, 3))
        .reshape(tok_rows, local * group * HD)
        .astype(jnp.bfloat16)
    )


def solution(mesh):
    placed = (
        P("seq", "tp"),
        P(),
        P("seq", "tp"),
        P(None, "seq", "tp"),
        P("seq", "tp"),
        P("seq"),
        P(),
    )
    return jax.shard_map(
        per_device, mesh=mesh, in_specs=placed, out_specs=P("seq", "tp"), check_vma=False
    )
```

profile of v0, /device:TPU:1, one launch (start us, length us, event | category | flops | bytes accessed | tf_op | source)
XLA Modules:
  0.0 596.8 jit_solution(13847445615156697512)
XLA Ops:
  8.7 61.9 %all_gather.13 = bf16[8,4096]{1,0:T(8,128)(2,1)S(1)} all-gather(bf16[8,512]{1,0:T(8,128)(2,1)} %param.13), channel_id=1, replica_groups=mesh['seq'=64,'tp'=8] {'tp'}, dimensions={1}, use_global_device_ids=true | all-gather | bytes 73728 | tf_op jit(solution)/shard_map/all_gather | solution.py:38
  73.1 30.0 %all-gather.4.cloned.1.call-done = bf16[128,4096]{1,0:T(8,128)(2,1)} async-done(((bf16[128,512]{1,0:T(8,128)(2,1)}), bf16[128,4096]{1,0:T(8,128)(2,1)}) %all-gather.4.cloned.1.call-update) | async-done | bytes 1048592 | tf_op jit(solution)/shard_map/all_gather | solution.py:37
  103.1 1.5 fusion.17
  104.6 1.6 fusion.19
  106.2 118.0 %all-gather.6.cloned.1.call-done = bf16[4096,768]{1,0:T(8,128)(2,1)} async-done(((bf16[64,768]{1,0:T(8,128)(2,1)}), bf16[4096,768]{1,0:T(8,128)(2,1)}) %all-gather.6.cloned.1.call-update) | async-done | bytes 6291472 | tf_op jit(solution)/shard_map/all_gather | solution.py:49
  224.2 3.8 fusion.20
  231.8 119.8 %all-gather.8.cloned.1.call-done = bf16[2,12288,128]{2,1,0:T(8,128)(2,1)} async-done(((bf16[2,192,128]{2,1,0:T(8,128)(2,1)}), bf16[2,12288,128]{2,1,0:T(8,128)(2,1)}) %all-gather.8.cloned.1.call-update) | async-done | bytes 6291472 | tf_op jit(solution)/shard_map/all_gather | solution.py:114
  351.6 237.6 %while.17 = (s32[]{:T(128)}, f32[1,4,128]{2,1,0:T(4,128)S(1)}, f32[1,4,128]{2,1,0:T(4,128)S(1)}, f32[1,4,128,128]{3,2,1,0:T(8,128)S(1)}, s32[64]{0:T(128)S(1)}, ...) while((s32[]{:T(128)}, f32[1,4,128]{2,1,0:T(4,128)S(1)}, ...), condition=%wide.region_7.8_spmd.clone, body=%wide.region_4.7_spmd.clone.sunk | while | flops 51471684 | bytes 2264493 | solution.py:123
  353.7 0.9 dynamic-slice_bitcast_fusion.2
  357.4 0.9 dynamic-slice_bitcast_fusion.2
  361.2 0.9 dynamic-slice_bitcast_fusion.2
  368.6 0.9 dynamic-slice_bitcast_fusion.2
  379.7 0.9 dynamic-slice_bitcast_fusion.2
  383.4 0.9 dynamic-slice_bitcast_fusion.2
  387.1 0.9 dynamic-slice_bitcast_fusion.2
  394.6 0.9 dynamic-slice_bitcast_fusion.2
  398.3 0.9 dynamic-slice_bitcast_fusion.2
  402.0 0.9 dynamic-slice_bitcast_fusion.2
  413.1 0.9 dynamic-slice_bitcast_fusion.2
  416.9 0.9 dynamic-slice_bitcast_fusion.2
  420.6 0.9 dynamic-slice_bitcast_fusion.2
  431.7 0.9 dynamic-slice_bitcast_fusion.2
  435.4 0.9 dynamic-slice_bitcast_fusion.2
  439.1 0.9 dynamic-slice_bitcast_fusion.2
  450.3 0.9 dynamic-slice_bitcast_fusion.2
  454.0 0.9 dynamic-slice_bitcast_fusion.2
  457.7 0.9 dynamic-slice_bitcast_fusion.2
  465.1 0.9 dynamic-slice_bitcast_fusion.2
  468.9 0.9 dynamic-slice_bitcast_fusion.2
  472.6 0.9 dynamic-slice_bitcast_fusion.2
  483.7 0.9 dynamic-slice_bitcast_fusion.2
  487.4 0.9 dynamic-slice_bitcast_fusion.2
  491.1 0.9 dynamic-slice_bitcast_fusion.2
  502.3 0.9 dynamic-slice_bitcast_fusion.2
  506.0 0.9 dynamic-slice_bitcast_fusion.2
  509.7 0.9 dynamic-slice_bitcast_fusion.2
  520.8 0.9 dynamic-slice_bitcast_fusion.2
  524.6 0.9 dynamic-slice_bitcast_fusion.2
  528.3 0.9 dynamic-slice_bitcast_fusion.2
  535.7 0.9 dynamic-slice_bitcast_fusion.2
  539.4 0.9 dynamic-slice_bitcast_fusion.2
  543.1 0.9 dynamic-slice_bitcast_fusion.2
  554.3 0.9 dynamic-slice_bitcast_fusion.2
  558.0 0.9 dynamic-slice_bitcast_fusion.2
  561.7 0.9 dynamic-slice_bitcast_fusion.2
  572.8 0.9 dynamic-slice_bitcast_fusion.2
  576.5 0.9 dynamic-slice_bitcast_fusion.2
  580.3 0.9 dynamic-slice_bitcast_fusion.2
  (766 shorter events, 163.6 us)
Async XLA Ops:
  6.5 96.6 %all-gather.4.cloned.1.call-start = ((), (), s32[]{:S(2)}) async-start(), calls=%async_computation | async-start | bytes 1179648 | tf_op jit(solution)/shard_map/all_gather | solution.py:37
  7.3 217.0 %all-gather.6.cloned.1.call-start = ((), (), s32[]{:S(2)}) async-start(), calls=%async_computation.1 | async-start | bytes 6389760 | tf_op jit(solution)/shard_map/all_gather | solution.py:49
  8.0 343.6 %all-gather.8.cloned.1.call-start = ((), (), s32[]{:S(2)}) async-start(), calls=%async_computation.2 | async-start | bytes 6389760 | tf_op jit(solution)/shard_map/all_gather | solution.py:114
Sparse Core Ops, SparseCore 0:
  10.4 92.6 all-gather.3
  105.3 118.9 all-gather.5
  231.1 120.5 all-gather.7
where the time goes:
time: 608 us; the launch traced here: 597 us
  waiting for transfers between devices  269 us (44%)
  local copies, waits for them, and re-layouts  98.4 us (16%)
  other arithmetic  68.7 us (11%)
  blocking collectives  61.9 us (10%)
  loops' own time  46.1 us (8%)
  matrix products  38.3 us (6%)
  between operations  13.9 us (2%)
    all_gather x1, waiting for transfers between devices, per_device(): piece = lax.all_gather(held, 'seq', axis=1, tiled=True)  120 us
    all_gather x1, waiting for transfers between devices, per_device(): full = add_rows(stacked, lax.all_gather(w_qkv, 'seq', axis=0, tiled=True))  118 us
    dynamic_slice x128, local copies, waits for them, and re-layouts, per_device(): lax.scan(step, carry, (jnp.arange(shards, dtype=jnp.int32), pieces))  95.8 us
    all_gather x1, blocking collectives, per_device(): lax.all_gather(recomp_hidden, 'tp', axis=1, tiled=True)  61.9 us
    another operation x1, loops' own time, per_device(): lax.scan(step, carry, (jnp.arange(shards, dtype=jnp.int32), pieces))  46.1 us
    lt x64, other arithmetic, attend_one(): cache_pos < begin  42.7 us
    all_gather x1, waiting for transfers between devices, per_device(): lax.all_gather(stream_x, 'tp', axis=1, tiled=True)  30 us
    dot_general x64, matrix products, attend_one(): jnp.einsum('kgtn,nkd->kgtd', weights.astype(jnp.bfloat16), value_rows, pr...  19.9 us
  transfers between devices with their start and end apart: 3, of which 3 were waited for; matrix products, arithmetic and copies ran while one was open for 1% of the time, Pallas kernels for 0%

commit v1 on v0

v1 whole, which is shorter than its diff:
```python
import functools
import math

import jax
import jax.numpy as jnp
from jax import lax
from jax.experimental import pallas as pl
from jax.experimental.pallas import tpu as pltpu
from jax.sharding import PartitionSpec as P

HEADS = 32
KVH = 8
HD = 128
GROUP = HEADS // KVH
NX, NZ, NC = 4, 8, 2
NY, NH = 4, 2
MESH = pl.DeviceIdType.MESH
F32 = jnp.float32
BF16 = jnp.bfloat16
LOW = -1e30
SCALE = 1.0 / math.sqrt(HD)


class Gather:
    def __init__(self, buf, recv, side, zsend, xsend, csend):
        self.buf, self.recv, self.side = buf, recv, side
        self.zsend, self.xsend, self.csend = zsend, xsend, csend
        s = lax.axis_index("seq")
        self.x, self.z, self.c = s // (NZ * NC), (s // NC) % NZ, s % NC

    def dev(self, x, z, c):
        return ((x + NX) % NX) * (NZ * NC) + z * NC + c

    def column(self, o):
        return (self.x + o // 2 + (o % 2) * (3 - 2 * (o // 2))) % NX

    def ok(self, t, g):
        j = self.z + (2 * g - 1) * t
        return (t >= 0) & (t + g >= 0) & (t < NZ) & (j >= 0) & (j < NZ) & ((t > 0) | (g == 0))

    def copy(self, block, send, recv, target):
        return pltpu.make_async_remote_copy(
            src_ref=self.buf.at[block],
            dst_ref=self.buf.at[block],
            send_sem=send,
            recv_sem=recv,
            device_id={"seq": target},
            device_id_type=MESH,
        )

    def to_side(self, block, o, t, g):
        self.copy(block, self.csend, self.side.at[o, t, g], self.dev(self.x, self.z, 1 - self.c)).start()

    def wait(self, sems, block, o, t, g):
        self.copy(block, self.csend, sems.at[o, t, g], self.dev(self.x, self.z, 1 - self.c)).wait_recv()

    def first(self):
        block = self.dev(self.x, self.z, self.c)

        @pl.when(self.z < NZ - 1)
        def _():
            self.copy(block, self.zsend, self.recv.at[0, 1, 0], self.dev(self.x, self.z + 1, self.c)).start()

        @pl.when(self.z > 0)
        def _():
            self.copy(block, self.zsend, self.recv.at[0, 1, 1], self.dev(self.x, self.z - 1, self.c)).start()

        self.spread(block, 0, 0)

    def spread(self, block, t, g):
        self.copy(block, self.xsend, self.recv.at[1, t, g], self.dev(self.x + 1, self.z, self.c)).start()
        self.copy(block, self.xsend, self.recv.at[2, t, g], self.dev(self.x - 1, self.z, self.c)).start()
        self.to_side(block, 0, t, g)

    def stage_a(self, t, g):
        d = 2 * g - 1

        @pl.when(self.ok(t, g) & (t > 0))
        def _():
            block = self.dev(self.x, self.z + d * t, self.c)
            self.wait(self.recv, block, 0, t, g)
            after = self.z - d

            @pl.when((after >= 0) & (after < NZ))
            def _():
                self.copy(block, self.zsend, self.recv.at[0, t + 1, g], self.dev(self.x, after, self.c)).start()

            self.spread(block, t, g)

    def stage_b(self, t, g):
        d = 2 * g - 1

        @pl.when(self.ok(t, g))
        def _():
            even = (t + g) % 2 == 0
            left = self.dev(self.x - 1, self.z + d * t, self.c)
            self.wait(self.recv, left, 1, t, g)

            @pl.when(even)
            def _():
                self.copy(left, self.xsend, self.recv.at[3, t, g], self.dev(self.x + 1, self.z, self.c)).start()

            self.to_side(left, 1, t, g)
            right = self.dev(self.x + 1, self.z + d * t, self.c)
            self.wait(self.recv, right, 2, t, g)

            @pl.when(jnp.logical_not(even))
            def _():
                self.copy(right, self.xsend, self.recv.at[3, t, g], self.dev(self.x - 1, self.z, self.c)).start()

            self.to_side(right, 2, t, g)

    def stage_c(self, t, g):
        d = 2 * g - 1

        @pl.when(self.ok(t, g))
        def _():
            far = self.dev(self.x + 2, self.z + d * t, self.c)
            self.wait(self.recv, far, 3, t, g)
            self.to_side(far, 3, t, g)

    def wait_side(self, x, o, t, g):
        self.wait(self.side, self.dev(x, self.z + (2 * g - 1) * t, 1 - self.c), o, t, g)

    def finish_sends(self):
        def done(sem, count):
            pltpu.make_async_remote_copy(
                src_ref=self.buf.at[pl.ds(0, count)],
                dst_ref=self.buf.at[pl.ds(0, count)],
                send_sem=sem,
                recv_sem=self.recv.at[0, 0, 0],
                device_id={"seq": self.dev(self.x, self.z, 1 - self.c)},
                device_id_type=MESH,
            ).wait_send()

        done(self.xsend, 3 * NZ)
        done(self.csend, 4 * NZ)
        inner = (self.z > 0) & (self.z < NZ - 1)

        @pl.when(inner)
        def _():
            done(self.zsend, NZ + 1)

        @pl.when(jnp.logical_not(inner))
        def _():
            done(self.zsend, 1)


def kernel(
    prefix_ref, x_ref, h_ref, gain_ref, w_ref, cache_ref, index_ref, cos_ref, sin_ref,
    out_ref,
    xbuf, wbuf, kvbuf, nx, proj, qs, top, total, accum,
    xrecv, xsend, wrecv, wside, krecv, kside, sends,
):
    s = lax.axis_index("seq")
    tp = lax.axis_index("tp")
    c = s % NC
    y, h = tp % NY, tp // NY
    toks, redo = x_ref.shape[0], h_ref.shape[0]
    rows = xbuf.shape[1]
    cached = cache_ref.shape[1]
    gw = Gather(wbuf, wrecv, wside, sends.at[0], sends.at[1], sends.at[2])
    gk = Gather(kvbuf, krecv, kside, sends.at[3], sends.at[4], sends.at[5])
    x, z = gw.x, gw.z

    barrier = pltpu.get_barrier_semaphore()

    def hello(axis, target):
        pl.semaphore_signal(barrier, inc=1, device_id={axis: target}, device_id_type=MESH)

    y_right, y_left = h * NY + (y + 1) % NY, h * NY + (y + NY - 1) % NY
    over = (1 - h) * NY + y
    hello("seq", gw.dev(x + 1, z, c))
    hello("seq", gw.dev(x - 1, z, c))
    hello("seq", gw.dev(x, z, 1 - c))
    hello("tp", y_right)
    hello("tp", y_left)
    hello("tp", over)

    @pl.when(z > 0)
    def _():
        hello("seq", gw.dev(x, z - 1, c))

    @pl.when(z < NZ - 1)
    def _():
        hello("seq", gw.dev(x, z + 1, c))

    wbuf[s] = w_ref[...]
    xbuf[tp, pl.ds(0, toks)] = x_ref[...]
    xbuf[tp, pl.ds(toks, rows - toks)] = jnp.concatenate(
        [h_ref[...], jnp.zeros((rows - toks - redo, h_ref.shape[1]), BF16)], 0
    )

    @pl.when((z > 0) & (z < NZ - 1))
    def _():
        pl.semaphore_wait(barrier, 8)

    @pl.when((z == 0) | (z == NZ - 1))
    def _():
        pl.semaphore_wait(barrier, 7)

    def xcopy(piece, slot, target):
        return pltpu.make_async_remote_copy(
            src_ref=xbuf.at[piece],
            dst_ref=xbuf.at[piece],
            send_sem=xsend.at[slot],
            recv_sem=xrecv.at[slot],
            device_id={"tp": target},
            device_id_type=MESH,
        )

    other = (1 - h) * NY
    y2 = (y + 2) % NY
    xcopy(tp, 0, over).start()
    xcopy(tp, 1, y_right).start()
    xcopy(tp, 2, y_left).start()
    gw.first()

    def near_x():
        xcopy(y_left, 1, y_right).wait_recv()
        xcopy(y_left, 3, y_right).start()
        xcopy(y_right, 2, y_left).wait_recv()

    def over_x():
        xcopy(over, 0, over).wait_recv()
        xcopy(over, 4, y_right).start()
        xcopy(over, 5, y_left).start()

    def far_x():
        right = other + (y + 1) % NY
        xcopy(right, 5, y_left).wait_recv()
        xcopy(right, 6, y_left).start()
        xcopy(other + (y + NY - 1) % NY, 4, y_right).wait_recv()

    def last_x():
        xcopy(h * NY + y2, 3, y_right).wait_recv()
        xcopy(other + y2, 6, y_left).wait_recv()

    @pl.loop(0, NZ + 2)
    def _(t):
        for step, part in ((2, near_x), (4, over_x), (6, far_x)):
            pl.when(t == step)(part)

        @pl.loop(0, 2)
        def _(g):
            gw.stage_a(t, g)
            gw.stage_b(t - 1, g)
            gw.stage_c(t - 2, g)

    last_x()

    feats = xbuf.shape[2]
    square = jnp.zeros((rows, 1), F32)
    for piece in range(NY * NH):
        values = xbuf[piece].astype(F32)
        square = square + jnp.sum(values * values, axis=-1, keepdims=True)
    factor = lax.rsqrt(square * (1.0 / (feats * NY * NH)) + 1e-05)
    for piece in range(NY * NH):
        span = pl.ds(piece * feats, feats)
        values = xbuf[piece].astype(F32)
        nx[:, span] = (values * factor * gain_ref[:, span]).astype(BF16)

    @pl.loop(0, NZ)
    def _(t):
        @pl.loop(0, 2)
        def _(g):
            @pl.when(gw.ok(t, g))
            def _():
                gw.wait_side(x, 0, t, g)
                gw.wait_side(x - 1, 1, t, g)
                gw.wait_side(x + 1, 2, t, g)
                gw.wait_side(x + 2, 3, t, g)

    per = 8
    wrows = wbuf.shape[1]
    cols = wbuf.shape[2]
    proj[...] = jnp.zeros_like(proj)

    @pl.loop(0, (NX * NZ * NC) // per)
    def _(k):
        weights = wbuf[pl.ds(k * per, per)].reshape(per * wrows, cols)
        left = nx[:, pl.ds(pl.multiple_of(k * per * wrows, per * wrows), per * wrows)]
        proj[...] += jnp.dot(left, weights, preferred_element_type=F32)

    cosine, sine = cos_ref[...], sin_ref[...]

    def rotate(v, n):
        return v * cosine[:n] + pltpu.roll(v, HD // 2, 1) * sine[:n]

    for head in range(GROUP):
        qs[pl.ds(head * toks, toks)] = rotate(proj[pl.ds(0, toks), pl.ds(head * HD, HD)], toks).astype(BF16)
    keys = rotate(proj[:, pl.ds(GROUP * HD, HD)], rows).astype(BF16)
    values = proj[:, pl.ds((GROUP + 1) * HD, HD)].astype(BF16)
    extra = rows - toks
    hit = lax.broadcasted_iota(jnp.int32, (cached, extra), 0) == index_ref[...]
    pick = hit.astype(BF16)
    changed = jnp.sum(hit.astype(F32), axis=1, keepdims=True) > 0.0
    for kind, new in ((0, keys), (1, values)):
        base = kind * (toks + cached)
        kvbuf[s, pl.ds(base, toks)] = new[:toks]
        moved = jnp.dot(pick, new[toks:], preferred_element_type=F32).astype(BF16)
        kvbuf[s, pl.ds(base + toks, cached)] = jnp.where(changed, moved, cache_ref[kind])

    gk.first()

    begin = prefix_ref[0]
    half = toks + cached

    def attend(key, value, bias):
        n = key.shape[0]
        for head in range(GROUP):
            span = pl.ds(head * toks, toks)
            score = lax.dot_general(
                qs[span], key, (((1,), (1,)), ((), ())), preferred_element_type=F32
            ) * SCALE + bias
            top_old = top[span]
            top_new = jnp.maximum(top_old, jnp.max(score, axis=1, keepdims=True))
            keep = jnp.exp(top_old - top_new)
            weights = jnp.exp(score - top_new[:, :1])
            top[span] = top_new
            total[span] = total[span] * keep + jnp.sum(weights, axis=1, keepdims=True)
            accum[span] = accum[span] * keep + jnp.dot(
                weights.astype(BF16), value, preferred_element_type=F32
            )

    top[...] = jnp.full_like(top, LOW)
    total[...] = jnp.zeros_like(total)
    accum[...] = jnp.zeros_like(accum)

    def one_device(d, stream_ok):
        place = lax.broadcasted_iota(jnp.int32, (toks, half), 1)
        cache_ok = (d * cached + place - toks) < begin
        allowed = ((place < toks) & stream_ok(place)) | ((place >= toks) & cache_ok)
        attend(kvbuf[d, pl.ds(0, half)], kvbuf[d, pl.ds(half, half)], jnp.where(allowed, 0.0, LOW))

    one_device(s, lambda place: place <= lax.broadcasted_iota(jnp.int32, (toks, half), 0))

    def sibling():
        d = gk.dev(x, z, 1 - c)
        gk.wait_side(x, 0, 0, 0)
        one_device(d, lambda place: place < c * toks)

    def parts(chip, base):
        return (
            kvbuf[2 * chip, pl.ds(base, toks)],
            kvbuf[2 * chip + 1, pl.ds(base, toks)],
            kvbuf[2 * chip, pl.ds(base + toks, cached)],
            kvbuf[2 * chip + 1, pl.ds(base + toks, cached)],
        )

    def one_chip(t, g):
        j = z + (2 * g - 1) * t

        @pl.loop(0, NX)
        def _(o):
            @pl.when((o > 0) | (t > 0))
            def _():
                col = gk.column(o)
                gk.wait_side(col, o, t, g)
                chip = col * NZ + j
                seen = chip < x * NZ + z
                place = lax.broadcasted_iota(jnp.int32, (1, 2 * cached), 1) + chip * 2 * cached
                bias = jnp.where(place < begin, 0.0, LOW)

                @pl.when(seen)
                def _():
                    attend(
                        jnp.concatenate(parts(chip, 0), 0),
                        jnp.concatenate(parts(chip, half), 0),
                        jnp.concatenate([jnp.zeros((1, 2 * toks), F32), bias], 1),
                    )

                @pl.when(jnp.logical_not(seen))
                def _():
                    attend(
                        jnp.concatenate(parts(chip, 0)[2:], 0),
                        jnp.concatenate(parts(chip, half)[2:], 0),
                        bias,
                    )

    @pl.loop(0, NZ + 3)
    def _(t):
        @pl.when(t == 1)
        def _():
            sibling()

        @pl.loop(0, 2)
        def _(g):
            gk.stage_a(t, g)
            gk.stage_b(t - 1, g)
            gk.stage_c(t - 2, g)

            @pl.when(gk.ok(t - 3, g))
            def _():
                one_chip(t - 3, g)

    for head in range(GROUP):
        span = pl.ds(head * toks, toks)
        out_ref[:, pl.ds(head * HD, HD)] = (accum[span] / total[span]).astype(BF16)

    gw.finish_sends()
    gk.finish_sends()
    for slot in range(7):
        xcopy(tp, slot, over).wait_send()


def per_device(stream_x, norm_gain, w_qkv, cache_kv, recomp_hidden, recomp_index, prefix_len):
    toks, redo = stream_x.shape[0], recomp_hidden.shape[0]
    feats = stream_x.shape[1]
    cached = cache_kv.shape[1]
    seqs = NX * NZ * NC
    rows = toks + 16
    seq_at = lax.axis_index("seq")
    token_ids = seq_at * toks + jnp.arange(toks, dtype=jnp.int32)
    pad = jnp.zeros((rows - toks - redo,), jnp.int32)
    places = jnp.concatenate([token_ids + prefix_len[0], recomp_index, pad]).astype(F32)
    freq = jnp.exp(-math.log(1000000.0) * jnp.arange(HD // 2, dtype=F32) * 2.0 / HD)
    angle = places[:, None] * freq[None, :]
    cosine, sine = jnp.cos(angle), jnp.sin(angle)
    cosine = jnp.concatenate([cosine, cosine], 1)
    sine = jnp.concatenate([-sine, sine], 1)
    index = jnp.concatenate([recomp_index - seq_at * cached, pad - 1])[None, :]
    vmem = pl.BlockSpec(memory_space=pltpu.VMEM)
    return pl.pallas_call(
        kernel,
        out_shape=jax.ShapeDtypeStruct((toks, GROUP * HD), BF16),
        in_specs=[pl.BlockSpec(memory_space=pltpu.SMEM)] + [vmem] * 8,
        out_specs=vmem,
        scratch_shapes=[
            pltpu.VMEM((NY * NH, rows, feats), BF16),
            pltpu.VMEM((seqs,) + w_qkv.shape, BF16),
            pltpu.VMEM((seqs, 2 * (toks + cached), HD), BF16),
            pltpu.VMEM((rows, NY * NH * feats), BF16),
            pltpu.VMEM((rows, w_qkv.shape[1]), F32),
            pltpu.VMEM((GROUP * toks, HD), BF16),
            pltpu.VMEM((GROUP * toks, HD), F32),
            pltpu.VMEM((GROUP * toks, HD), F32),
            pltpu.VMEM((GROUP * toks, HD), F32),
            pltpu.SemaphoreType.DMA((7,)),
            pltpu.SemaphoreType.DMA((7,)),
            pltpu.SemaphoreType.DMA((4, NZ + 1, 2)),
            pltpu.SemaphoreType.DMA((4, NZ + 1, 2)),
            pltpu.SemaphoreType.DMA((4, NZ + 1, 2)),
            pltpu.SemaphoreType.DMA((4, NZ + 1, 2)),
            pltpu.SemaphoreType.DMA((6,)),
        ],
        compiler_params=pltpu.CompilerParams(
            collective_id=0, has_side_effects=True, vmem_limit_bytes=50 * 1024 * 1024
        ),
    )(
        prefix_len,
        stream_x,
        recomp_hidden,
        norm_gain[None, :],
        w_qkv,
        cache_kv,
        index,
        cosine,
        sine,
    )


def solution(mesh):
    placed = (
        P("seq", "tp"),
        P(),
        P("seq", "tp"),
        P(None, "seq", "tp"),
        P("seq", "tp"),
        P("seq"),
        P(),
    )
    return jax.shard_map(
        per_device, mesh=mesh, in_specs=placed, out_specs=P("seq", "tp"), check_vma=False
    )
```

time: 608 us -> 147 us (0.24)
  the two profiles are of different devices: /device:TPU:1 before, /device:TPU:30 now
where the time goes in v1:
time: 147 us
  Pallas kernels  144 us (98%)
  local copies, waits for them, and re-layouts  2.13 us (1%)
    pallas_call x1, Pallas kernels, per_device(): pl.pallas_call(kernel, out_shape=jax.ShapeDtypeStruct((toks, GROUP * HD),...  144 us

profile of v1, /device:TPU:30, one launch (start us, length us, event | category | flops | bytes accessed | tf_op | source)
XLA Modules:
  0.0 147.2 jit_solution(12619018801572274696)
XLA Ops:
  0.7 0.0 copy-start.5
  0.7 0.6 copy-done.5
  1.3 0.1 add_convert_fusion
  1.4 0.3 fusion
  1.8 0.0 copy-start
  1.8 0.0 copy-start.1
  1.8 0.0 copy-start.2
  1.8 0.0 copy-start.3
  1.8 0.0 copy-start.4
  1.8 0.1 pad_maximum_fusion
  1.9 0.7 copy-done
  2.7 0.1 copy-done.1
  2.7 0.0 copy-done.2
  2.7 0.0 copy-done.3
  2.7 0.0 copy-done.4
  2.7 143.8 %shard_map.73 = bf16[128,512]{1,0:T(8,128)(2,1)S(1)} custom-call(s32[1]{0:T(128)} %copy.9.prefix_ref, bf16[128,512]{1,0:T(8,128)(2,1)S(1)} %copy-done, bf16[8,512]{1,0:T(8,128)(2,1)S(1)} %copy-done.4, f32[1,4096]{1,0:T(1,128)S(1)} %bitcast.5, bf16[64,768]{1,0:T(8,128)(2,1)S(1)} %copy-done.1, bf16[2,64,128]{2,1,0:T(8,128)(2,1)S(1)} %copy-done.2, ...), custom_call_target="tpu_custom_call" | custom-call | tf_op jit(solution)/shard_map/pallas_call | solution.py:424
  146.5 0.7 copy.10
  (5 shorter events, 0.0 us)
Async XLA Ops:
  0.7 0.7 copy-start.5
  1.8 0.9 copy-start
  1.8 0.9 copy-start.1
  1.8 0.9 copy-start.2
  1.8 0.9 copy-start.3
  1.8 0.9 copy-start.4
